TPU v7x, 32 devices: a whole 2x2x4 slice. The times are simulated.
32 devices in a mesh: sect: 2 (over x), seq: 4 (over y, core), dp: 4 (over z).
Axes of the slice: x: 2, y: 2, z: 4, core: 2. Of those that a mesh axis runs over, the one named last changes fastest.
Arguments:
- query_tiles: bfloat16 [4, 8, 128, 2048], P('dp', None, 'sect', 'seq'), may hold values from -6 to 6
- key_tiles: bfloat16 [4, 8, 128, 2048], P('dp', None, 'sect', 'seq'), may hold values from -6 to 6
- value_tiles: bfloat16 [4, 8, 128, 2048], P('dp', None, 'sect', 'seq'), may hold values from -6 to 6
- text_keys: bfloat16 [8, 256, 2048], P(('sect', 'dp'), 'seq'), may hold values from -6 to 6
- text_values: bfloat16 [8, 256, 2048], P(('sect', 'dp'), 'seq'), may hold values from -6 to 6
- text_lengths: int32 [8], P(('sect', 'dp')), may hold values from 32 to 256, as said below
- tile_place: int32 [4], replicated, may hold values from 0 to 3, each once
Outputs:
- attended: bfloat16 [8, 512, 2048], P(('sect', 'dp'), 'seq')
Inputs may be any that keep to these rules, and one draw needn't show every extreme that they name: `tile_place`: each spatial position is held by exactly one tile slot. `text_lengths`: the live text tokens of a clip are its first rows; some clip fills all 256 slots.
All inputs are finite; a program needn't handle non-finite values.
Results may differ from a plain program's by a relative error of at most 0.0031.
Values may be sent and summed in bfloat16 or wider, within the bound.
A program may use at most 64 MiB of HBM per device.

v0:
```python
import math
import jax
import jax.numpy as jnp
from jax import lax
from jax.sharding import PartitionSpec as P

HD = 128


def attend(queries_flat, keys_video, values_video, keys_text, values_text, length):
    query_rows, head_width = queries_flat.shape
    head_count = head_width // HD
    score_scale = 1.0 / math.sqrt(HD)
    keys_video = keys_video.reshape(-1, head_count, HD)
    values_video = values_video.reshape(-1, head_count, HD)
    keys_text = keys_text.reshape(-1, head_count, HD)
    values_text = values_text.reshape(-1, head_count, HD)
    live_mask = jnp.arange(keys_text.shape[0], dtype=jnp.int32) < length
    block_rows = math.gcd(query_rows, 512)

    def one_block(query_block):
        score_video = (
            jnp.einsum("qhd,khd->hqk", query_block, keys_video, preferred_element_type=jnp.float32)
            * score_scale
        )
        score_text = (
            jnp.einsum("qhd,khd->hqk", query_block, keys_text, preferred_element_type=jnp.float32)
            * score_scale
        )
        score_text = jnp.where(live_mask[None, None, :], score_text, -jnp.inf)
        row_max = jnp.maximum(jnp.max(score_video, axis=-1), jnp.max(score_text, axis=-1))[
            ..., None
        ]
        expo_video = jnp.exp(score_video - row_max)
        expo_text = jnp.exp(score_text - row_max)
        denominators = jnp.sum(expo_video, axis=-1) + jnp.sum(expo_text, axis=-1)
        mixed = jnp.einsum(
            "hqk,khd->qhd",
            expo_video.astype(jnp.bfloat16),
            values_video,
            preferred_element_type=jnp.float32,
        )
        mixed = mixed + jnp.einsum(
            "hqk,khd->qhd",
            expo_text.astype(jnp.bfloat16),
            values_text,
            preferred_element_type=jnp.float32,
        )
        return (mixed / jnp.transpose(denominators)[:, :, None]).astype(jnp.bfloat16)

    blocks = queries_flat.reshape(query_rows // block_rows, block_rows, head_count, HD)
    return lax.map(one_block, blocks).reshape(query_rows, head_width)


def shards(query_tiles, key_tiles, value_tiles, text_keys, text_values, text_lengths, tile_place):
    tile_count = lax.axis_size("dp")
    sect_count = lax.axis_size("sect")
    part_rows = query_tiles.shape[2]
    head_width = query_tiles.shape[3]
    tile_seq = part_rows * sect_count

    def regroup(piece):
        return piece.reshape(1, sect_count, tile_count, part_rows, head_width)

    relayed = (
        lax.all_to_all(
            lax.all_to_all(regroup(query_tiles), "sect", split_axis=1, concat_axis=3, tiled=True),
            "dp",
            split_axis=2,
            concat_axis=0,
            tiled=True,
        ),
        lax.all_to_all(
            lax.all_to_all(regroup(key_tiles), "sect", split_axis=1, concat_axis=3, tiled=True),
            "dp",
            split_axis=2,
            concat_axis=0,
            tiled=True,
        ),
        lax.all_to_all(
            lax.all_to_all(regroup(value_tiles), "sect", split_axis=1, concat_axis=3, tiled=True),
            "dp",
            split_axis=2,
            concat_axis=0,
            tiled=True,
        ),
    )
    spatial_order = jnp.argsort(tile_place)
    seq_count = lax.axis_size("seq")
    tile_rows = tile_seq // seq_count

    def arrange(piece):
        grid = piece.reshape(tile_count, seq_count, tile_rows, head_width)
        placed = jnp.take(grid, spatial_order, axis=0)
        placed = jnp.transpose(placed, (1, 0, 2, 3))
        return placed.reshape(seq_count * tile_count * tile_rows, head_width)

    video_queries = arrange(relayed[0])
    video_keys = arrange(relayed[1])
    video_values = arrange(relayed[2])
    keys_text, values_text = (
        lax.all_to_all(text_keys[0], "seq", split_axis=1, concat_axis=0, tiled=True),
        lax.all_to_all(text_values[0], "seq", split_axis=1, concat_axis=0, tiled=True),
    )
    attended_heads = attend(
        video_queries, video_keys, video_values, keys_text, values_text, text_lengths[0]
    )
    attended = lax.all_to_all(attended_heads, "seq", split_axis=0, concat_axis=1, tiled=True)
    return attended[None]


def solution(mesh):
    in_specs = (
        P("dp", None, "sect", "seq"),
        P("dp", None, "sect", "seq"),
        P("dp", None, "sect", "seq"),
        P(("sect", "dp"), "seq", None),
        P(("sect", "dp"), "seq", None),
        P(("sect", "dp")),
        P(),
    )
    out_specs = P(("sect", "dp"), "seq", None)
    return jax.shard_map(shards, mesh=mesh, in_specs=in_specs, out_specs=out_specs, check_vma=False)
```

profile of v0, /device:TPU:0, one launch (start us, length us, event | category | flops | bytes accessed | tf_op | source)
XLA Modules:
  0.0 116.4 jit_solution(8662692775523040408)
XLA Ops:
  0.0 0.0 copy-start
  0.0 0.0 copy-start.1
  0.0 1.2 %all_to_all.111 = bf16[64,4,512]{2,1,0:T(4,128)(2,1)S(1)} reshape(bf16[1,64,2048]{2,1,0:T(8,128)(2,1)} %param.12) | data formatting | bytes 524288 | tf_op jit(solution)/shard_map/all_to_all | solution.py:102
  1.2 0.7 copy.57
  2.0 4.2 %all-to-all-start.6 = ((bf16[64,4,512]{2,0,1:T(8,128)(2,1)}), bf16[64,4,512]{2,0,1:T(8,128)(2,1)S(1)}, u32[]{:S(2)}, u32[]{:S(2)}) async-start(bf16[64,4,512]{2,0,1:T(8,128)(2,1)} %copy.57), calls=%async_computation.6 | async-start | bytes 524288 | tf_op jit(solution)/shard_map/all_to_all | solution.py:102
  6.2 1.1 all_to_all.114
  7.4 4.8 %all-to-all-done.6 = bf16[64,4,512]{2,0,1:T(8,128)(2,1)S(1)} async-done(((bf16[64,4,512]{2,0,1:T(8,128)(2,1)}), bf16[64,4,512]{2,0,1:T(8,128)(2,1)S(1)}, u32[]{:S(2)}, u32[]{:S(2)}) %all-to-all-start.6) | async-done | bytes 262176 | tf_op jit(solution)/shard_map/all_to_all | solution.py:102
  12.3 8.4 %all_to_all.129 = bf16[64,4,512]{2,0,1:T(8,128)(2,1)S(1)} all-to-all(bf16[64,4,512]{2,0,1:T(8,128)(2,1)S(1)} %copy.62), channel_id=1, replica_groups=mesh['sect'=2,'seq'=4,'dp'=4] {'seq'}, dimensions={1} | all-to-all | bytes 524288 | tf_op jit(solution)/shard_map/all_to_all | solution.py:103
  20.7 0.0 copy-done
  20.7 10.7 %all_to_all.130 = bf16[1,2,4,64,512]{4,3,2,0,1:T(8,128)(2,1)S(1)} all-to-all(bf16[1,2,4,64,512]{4,3,2,0,1:T(8,128)(2,1)S(1)} %bitcast.72), channel_id=1, replica_groups=mesh['sect'=2,'seq'=4,'dp'=4] {'sect'}, dimensions={1} | all-to-all | bytes 1048576 | tf_op jit(solution)/shard_map/all_to_all | solution.py:67
  31.4 0.0 copy-done.1
  31.4 9.1 %all_to_all.131 = bf16[1,2,4,64,512]{4,3,2,0,1:T(8,128)(2,1)S(1)} all-to-all(bf16[1,2,4,64,512]{4,3,2,0,1:T(8,128)(2,1)S(1)} %bitcast.73), channel_id=1, replica_groups=mesh['sect'=2,'seq'=4,'dp'=4] {'sect'}, dimensions={1} | all-to-all | bytes 1048576 | tf_op jit(solution)/shard_map/all_to_all | solution.py:74
  40.5 3.5 %all-to-all-start = ((bf16[1,2,4,64,512]{4,3,2,0,1:T(8,128)(2,1)}), bf16[1,2,4,64,512]{4,3,2,0,1:T(8,128)(2,1)S(1)}, u32[]{:S(2)}, u32[]{:S(2)}) async-start(bf16[1,2,4,64,512]{4,3,2,0,1:T(8,128)(2,1)} %bitcast.1), calls=%async_computation | async-start | bytes 1048576 | tf_op jit(solution)/shard_map/all_to_all | solution.py:81
  44.0 0.8 copy.48
  44.8 5.7 %all-to-all-done = bf16[1,2,4,64,512]{4,3,2,0,1:T(8,128)(2,1)S(1)} async-done(((bf16[1,2,4,64,512]{4,3,2,0,1:T(8,128)(2,1)}), bf16[1,2,4,64,512]{4,3,2,0,1:T(8,128)(2,1)S(1)}, u32[]{:S(2)}, u32[]{:S(2)}) %all-to-all-start) | async-done | bytes 524320 | tf_op jit(solution)/shard_map/all_to_all | solution.py:81
  50.6 5.1 %all-to-all-start.3 = ((bf16[1,1,4,128,512]{4,3,1,0,2:T(8,128)(2,1)}), bf16[1,1,4,128,512]{4,3,1,0,2:T(8,128)(2,1)S(1)}, u32[]{:S(2)}, u32[]{:S(2)}) async-start(bf16[1,1,4,128,512]{4,3,1,0,2:T(8,128)(2,1)} %bitcast.13), calls=%async_computation.3 | async-start | bytes 1048576 | tf_op jit(solution)/shard_map/all_to_all | solution.py:66
  55.7 0.0 copy-start.3
  55.7 0.8 copy.52
  56.5 10.1 %all-to-all-done.3 = bf16[1,1,4,128,512]{4,3,1,0,2:T(8,128)(2,1)S(1)} async-done(((bf16[1,1,4,128,512]{4,3,1,0,2:T(8,128)(2,1)}), bf16[1,1,4,128,512]{4,3,1,0,2:T(8,128)(2,1)S(1)}, u32[]{:S(2)}, u32[]{:S(2)}) %all-to-all-start.3) | async-done | bytes 524320 | tf_op jit(solution)/shard_map/all_to_all | solution.py:66
  66.7 3.5 %all-to-all-start.5 = ((bf16[1,1,4,128,512]{4,3,1,0,2:T(8,128)(2,1)}), bf16[1,1,4,128,512]{4,3,1,0,2:T(8,128)(2,1)S(1)}, u32[]{:S(2)}, u32[]{:S(2)}) async-start(bf16[1,1,4,128,512]{4,3,1,0,2:T(8,128)(2,1)} %bitcast.21), calls=%async_computation.5 | async-start | bytes 1048576 | tf_op jit(solution)/shard_map/all_to_all | solution.py:73
  70.2 0.8 copy.44
  71.0 10.7 %all-to-all-done.5 = bf16[1,1,4,128,512]{4,3,1,0,2:T(8,128)(2,1)S(1)} async-done(((bf16[1,1,4,128,512]{4,3,1,0,2:T(8,128)(2,1)}), bf16[1,1,4,128,512]{4,3,1,0,2:T(8,128)(2,1)S(1)}, u32[]{:S(2)}, u32[]{:S(2)}) %all-to-all-start.5) | async-done | bytes 524320 | tf_op jit(solution)/shard_map/all_to_all | solution.py:73
  81.7 3.5 %all-to-all-start.1 = ((bf16[1,1,4,128,512]{4,3,1,0,2:T(8,128)(2,1)}), bf16[1,1,4,128,512]{4,3,1,0,2:T(8,128)(2,1)S(1)}, u32[]{:S(2)}, u32[]{:S(2)}) async-start(bf16[1,1,4,128,512]{4,3,1,0,2:T(8,128)(2,1)} %bitcast.5), calls=%async_computation.1 | async-start | bytes 1048576 | tf_op jit(solution)/shard_map/all_to_all | solution.py:80
  85.8 0.0 copy-done.3
  85.9 0.7 sort.17
  86.6 0.8 reshape.75
  87.4 0.1 reshape.76
  87.5 0.6 gather_fusion.1
  88.0 0.6 gather_fusion.2
  88.6 8.7 %all-to-all-done.1 = bf16[1,1,4,128,512]{4,3,1,0,2:T(8,128)(2,1)S(1)} async-done(((bf16[1,1,4,128,512]{4,3,1,0,2:T(8,128)(2,1)}), bf16[1,1,4,128,512]{4,3,1,0,2:T(8,128)(2,1)S(1)}, u32[]{:S(2)}, u32[]{:S(2)}) %all-to-all-start.1) | async-done | bytes 524320 | tf_op jit(solution)/shard_map/all_to_all | solution.py:80
  97.3 0.6 gather_fusion
  97.9 0.2 select_bitcast_fusion.2
  98.2 0.1 reshape_reshape.7
  98.4 0.1 squeeze.10
  98.5 0.1 reshape_reshape.8
  98.7 0.0 copy-start.2
  98.7 0.7 multiply_reduce_fusion
  99.4 0.2 copy-done.2
  99.6 0.5 fusion.6
  100.1 0.5 fusion.7
  100.6 0.7 convolution_bitcast_fusion
  101.3 0.7 fusion
  102.0 0.9 fusion.18
  103.0 0.1 all_to_all.117
  103.1 0.1 copy.66
  103.2 12.2 %all_to_all.132 = bf16[4,128,512]{1,2,0:T(8,128)(2,1)S(1)} all-to-all(bf16[4,128,512]{1,2,0:T(8,128)(2,1)S(1)} %copy.66), channel_id=1, replica_groups=mesh['sect'=2,'seq'=4,'dp'=4] {'seq'}, dimensions={0} | all-to-all | bytes 1048576 | tf_op jit(solution)/shard_map/all_to_all | solution.py:108
  115.4 1.0 copy.67
  (11 shorter events, 0.2 us)
Async XLA Ops:
  0.0 20.7 %copy-start = (bf16[1,8,64,512]{3,2,1,0:T(8,128)(2,1)S(1)}, bf16[1,8,64,512]{3,2,1,0:T(8,128)(2,1)}, u32[]{:S(2)}) copy-start(bf16[1,8,64,512]{3,2,1,0:T(8,128)(2,1)} %param.9) | copy-start | bytes 1572868
  0.0 31.4 %copy-start.1 = (bf16[1,8,64,512]{3,2,1,0:T(8,128)(2,1)S(1)}, bf16[1,8,64,512]{3,2,1,0:T(8,128)(2,1)}, u32[]{:S(2)}) copy-start(bf16[1,8,64,512]{3,2,1,0:T(8,128)(2,1)} %param.10) | copy-start | bytes 1572868
  2.0 10.3 %all-to-all-start.6 = ((bf16[64,4,512]{2,0,1:T(8,128)(2,1)}), bf16[64,4,512]{2,0,1:T(8,128)(2,1)S(1)}, u32[]{:S(2)}, u32[]{:S(2)}) async-start(bf16[64,4,512]{2,0,1:T(8,128)(2,1)} %copy.57), calls=%async_computation.6 | async-start | bytes 524288 | tf_op jit(solution)/shard_map/all_to_all | solution.py:102
  40.5 10.1 %all-to-all-start = ((bf16[1,2,4,64,512]{4,3,2,0,1:T(8,128)(2,1)}), bf16[1,2,4,64,512]{4,3,2,0,1:T(8,128)(2,1)S(1)}, u32[]{:S(2)}, u32[]{:S(2)}) async-start(bf16[1,2,4,64,512]{4,3,2,0,1:T(8,128)(2,1)} %bitcast.1), calls=%async_computation | async-start | bytes 1048576 | tf_op jit(solution)/shard_map/all_to_all | solution.py:81
  50.6 16.1 %all-to-all-start.3 = ((bf16[1,1,4,128,512]{4,3,1,0,2:T(8,128)(2,1)}), bf16[1,1,4,128,512]{4,3,1,0,2:T(8,128)(2,1)S(1)}, u32[]{:S(2)}, u32[]{:S(2)}) async-start(bf16[1,1,4,128,512]{4,3,1,0,2:T(8,128)(2,1)} %bitcast.13), calls=%async_computation.3 | async-start | bytes 1048576 | tf_op jit(solution)/shard_map/all_to_all | solution.py:66
  55.7 30.1 %copy-start.3 = (s32[4]{0:T(128)S(1)}, s32[4]{0:T(128)}, u32[]{:S(2)}) copy-start(s32[4]{0:T(128)} %param.15) | copy-start | bytes 52
  66.7 15.0 %all-to-all-start.5 = ((bf16[1,1,4,128,512]{4,3,1,0,2:T(8,128)(2,1)}), bf16[1,1,4,128,512]{4,3,1,0,2:T(8,128)(2,1)S(1)}, u32[]{:S(2)}, u32[]{:S(2)}) async-start(bf16[1,1,4,128,512]{4,3,1,0,2:T(8,128)(2,1)} %bitcast.21), calls=%async_computation.5 | async-start | bytes 1048576 | tf_op jit(solution)/shard_map/all_to_all | solution.py:73
  81.7 15.6 %all-to-all-start.1 = ((bf16[1,1,4,128,512]{4,3,1,0,2:T(8,128)(2,1)}), bf16[1,1,4,128,512]{4,3,1,0,2:T(8,128)(2,1)S(1)}, u32[]{:S(2)}, u32[]{:S(2)}) async-start(bf16[1,1,4,128,512]{4,3,1,0,2:T(8,128)(2,1)} %bitcast.5), calls=%async_computation.1 | async-start | bytes 1048576 | tf_op jit(solution)/shard_map/all_to_all | solution.py:80
  98.7 1.0 copy-start.2
where the time goes:
time: 117 us; the launch traced here: 116 us
  blocking collectives  40.4 us (35%)
  waiting for transfers between devices  40.1 us (34%)
  starting transfers between devices  19.8 us (17%)
  local copies, waits for them, and re-layouts  10.2 us (9%)
  matrix products  2.8 us (2%)
  other arithmetic  2.19 us (2%)
    all_to_all x1, blocking collectives, shards(): lax.all_to_all(attended_heads, 'seq', split_axis=0, concat_axis=1, tiled=...  12.2 us
    all_to_all x1, blocking collectives, shards(): lax.all_to_all(regroup(query_tiles), 'sect', split_axis=1, concat_axis=3,...  10.7 us
    all_to_all x1, waiting for transfers between devices, shards(): lax.all_to_all(lax.all_to_all(regroup(key_tiles), 'sect', split_axis=1, c...  10.7 us
    all_to_all x1, waiting for transfers between devices, shards(): lax.all_to_all(lax.all_to_all(regroup(query_tiles), 'sect', split_axis=1,...  10.1 us
    all_to_all x1, blocking collectives, shards(): lax.all_to_all(regroup(key_tiles), 'sect', split_axis=1, concat_axis=3, t...  9.08 us
    all_to_all x1, waiting for transfers between devices, shards(): lax.all_to_all(lax.all_to_all(regroup(value_tiles), 'sect', split_axis=1,...  8.71 us
    all_to_all x1, blocking collectives, shards(): lax.all_to_all(text_values[0], 'seq', split_axis=1, concat_axis=0, tiled=...  8.41 us
    all_to_all x1, waiting for transfers between devices, shards(): lax.all_to_all(regroup(value_tiles), 'sect', split_axis=1, concat_axis=3,...  5.72 us
  transfers between devices with their start and end apart: 5, of which 5 were waited for; matrix products, arithmetic and copies ran while one was open for 5% of the time, Pallas kernels for 0%

commit v1 on v0

--- a/solution.py
+++ b/solution.py
@@ -5,6 +5,28 @@
 from jax.sharding import PartitionSpec as P
 
 HD = 128
+
+
+def supply_all_the_page(row_data):
+    r2 = lax.axis_index("seq")
+    y2 = lax.axis_size("seq")
+    met_up, outcome_arr = (y2, r2)
+    part_next = list(row_data.shape)
+    carry_out = row_data.shape[1] // met_up
+    part_next[1] = carry_out
+    long_array = part_next[0]
+    part_next[0] = long_array * met_up
+    then = jnp.zeros(part_next, row_data.dtype)
+    for hop_no in [*range(met_up)]:
+        arr_now = lax.dynamic_slice_in_dim(
+            row_data, (outcome_arr ^ hop_no) * carry_out, carry_out, axis=1
+        )
+        if hop_no:
+            arr_now = lax.ppermute(arr_now, "seq", [(kk, kk ^ hop_no) for kk in range(met_up)])
+        then = lax.dynamic_update_slice_in_dim(
+            then, arr_now, (outcome_arr ^ hop_no) * long_array, axis=0
+        )
+    return then
 
 
 def attend(queries_flat, keys_video, values_video, keys_text, values_text, length):
@@ -100,7 +122,7 @@
     video_values = arrange(relayed[2])
     keys_text, values_text = (
         lax.all_to_all(text_keys[0], "seq", split_axis=1, concat_axis=0, tiled=True),
-        lax.all_to_all(text_values[0], "seq", split_axis=1, concat_axis=0, tiled=True),
+        supply_all_the_page(text_values[0]),
     )
     attended_heads = attend(
         video_queries, video_keys, video_values, keys_text, values_text, text_lengths[0]

time: 117 us -> 111 us (0.949)
  waiting for transfers between devices: 40.1 us -> 29.8 us
  blocking collectives: 40.4 us -> 43.1 us
  matrix products: 2.8 us -> 4.99 us
  starting transfers between devices: 19.8 us -> 17.9 us
  local copies, waits for them, and re-layouts: 10.2 us -> 11.8 us
    all_to_all x1, waiting for transfers between devices: 10.7 us -> 2.8 us  [shards(): lax.all_to_all(lax.all_to_all(regroup(key_tiles), 'sect', split_axis=1, c...]
    all_to_all x2 -> x1, waiting for transfers between devices: 10.6 us -> 5.72 us  [shards(): lax.all_to_all(regroup(key_tiles), 'sect', split_axis=1, concat_axis=3, t...]
    all_to_all x2 -> x1, starting transfers between devices: 7.73 us -> 3.49 us  [shards(): lax.all_to_all(regroup(key_tiles), 'sect', split_axis=1, concat_axis=3, t...]
    all_to_all x2, blocking collectives: 17.5 us -> 21.4 us  [the longest x1 11.4 us: shards(): lax.all_to_all(regroup(value_tiles), 'sect', split_axis=1, concat_axis=3,...]
    dynamic_update_slice x0 -> x4, local copies, waits for them, and re-layouts: none -> 2.64 us  [supply_all_the_page(): lax.dynamic_update_slice_in_dim(then, arr_now, (outcome_arr ^ hop_no) * l...]
    ppermute x0 -> x3, starting transfers between devices: none -> 2.59 us  [supply_all_the_page(): lax.ppermute(arr_now, 'seq', [(kk, kk ^ hop_no) for kk in range(met_up)])]
    dot_general x1, matrix products: 0.95 us -> 3.1 us  [one_block(): jnp.einsum('hqk,khd->qhd', expo_video.astype(jnp.bfloat16), values_video,...]
    all_to_all x1, starting transfers between devices: 5.14 us -> 3.47 us  [shards(): lax.all_to_all(lax.all_to_all(regroup(query_tiles), 'sect', split_axis=1,...]
  transfers between devices with their start and end apart: 5 -> 7, of which waited for: 5 -> 5; matrix products, arithmetic and copies ran while one was open for 5% -> 7% of each run, Pallas kernels for 0% -> 0%
where the time goes in v1:
time: 111 us
  blocking collectives  43.1 us (39%)
  waiting for transfers between devices  29.8 us (27%)
  starting transfers between devices  17.9 us (16%)
  local copies, waits for them, and re-layouts  11.8 us (11%)
  matrix products  4.99 us (4%)
  other arithmetic  2.26 us (2%)
    all_to_all x1, blocking collectives, shards(): lax.all_to_all(attended_heads, 'seq', split_axis=0, concat_axis=1, tiled=...  12.3 us
    all_to_all x1, blocking collectives, shards(): lax.all_to_all(regroup(value_tiles), 'sect', split_axis=1, concat_axis=3,...  11.4 us
    all_to_all x1, waiting for transfers between devices, shards(): lax.all_to_all(lax.all_to_all(regroup(query_tiles), 'sect', split_axis=1,...  10.8 us
    all_to_all x1, waiting for transfers between devices, shards(): lax.all_to_all(lax.all_to_all(regroup(value_tiles), 'sect', split_axis=1,...  10.3 us
    all_to_all x1, blocking collectives, shards(): lax.all_to_all(text_keys[0], 'seq', split_axis=1, concat_axis=0, tiled=True)  10.1 us
    all_to_all x1, blocking collectives, shards(): lax.all_to_all(regroup(query_tiles), 'sect', split_axis=1, concat_axis=3,...  9.36 us
    all_to_all x1, waiting for transfers between devices, shards(): lax.all_to_all(regroup(key_tiles), 'sect', split_axis=1, concat_axis=3, t...  5.72 us
    all_to_all x1, starting transfers between devices, shards(): lax.all_to_all(lax.all_to_all(regroup(value_tiles), 'sect', split_axis=1,...  4.87 us
  transfers between devices with their start and end apart: 7, of which 5 were waited for; matrix products, arithmetic and copies ran while one was open for 7% of the time, Pallas kernels for 0%

profile of v1, /device:TPU:0, one launch (start us, length us, event | category | flops | bytes accessed | tf_op | source)
XLA Modules:
  0.0 110.9 jit_solution(8525421022184524324)
XLA Ops:
  0.0 0.0 copy-start.1
  0.0 1.2 %all_to_all.99 = bf16[64,4,512]{2,1,0:T(4,128)(2,1)S(1)} reshape(bf16[1,64,2048]{2,1,0:T(8,128)(2,1)} %param.12) | data formatting | bytes 524288 | tf_op jit(solution)/shard_map/all_to_all | solution.py:124
  1.3 10.1 %all_to_all.113 = bf16[64,4,512]{2,0,1:T(8,128)(2,1)S(1)} all-to-all(bf16[64,4,512]{2,0,1:T(8,128)(2,1)S(1)} %copy.58), channel_id=1, replica_groups=mesh['sect'=2,'seq'=4,'dp'=4] {'seq'}, dimensions={1} | all-to-all | bytes 524288 | tf_op jit(solution)/shard_map/all_to_all | solution.py:124
  11.3 11.4 %all_to_all.114 = bf16[1,2,4,64,512]{4,3,2,0,1:T(8,128)(2,1)S(1)} all-to-all(bf16[1,2,4,64,512]{4,3,2,0,1:T(8,128)(2,1)} %bitcast.76), channel_id=1, replica_groups=mesh['sect'=2,'seq'=4,'dp'=4] {'sect'}, dimensions={1} | all-to-all | bytes 1048576 | tf_op jit(solution)/shard_map/all_to_all | solution.py:103
  22.7 0.0 copy-done.1
  22.7 9.4 %all_to_all.115 = bf16[1,2,4,64,512]{4,3,2,0,1:T(8,128)(2,1)S(1)} all-to-all(bf16[1,2,4,64,512]{4,3,2,0,1:T(8,128)(2,1)S(1)} %bitcast.77), channel_id=1, replica_groups=mesh['sect'=2,'seq'=4,'dp'=4] {'sect'}, dimensions={1} | all-to-all | bytes 1048576 | tf_op jit(solution)/shard_map/all_to_all | solution.py:89
  32.1 3.5 %all-to-all-start.4 = ((bf16[1,2,4,64,512]{4,3,2,0,1:T(8,128)(2,1)}), bf16[1,2,4,64,512]{4,3,2,0,1:T(8,128)(2,1)S(1)}, u32[]{:S(2)}, u32[]{:S(2)}) async-start(bf16[1,2,4,64,512]{4,3,2,0,1:T(8,128)(2,1)} %bitcast.17), calls=%async_computation.4 | async-start | bytes 1048576 | tf_op jit(solution)/shard_map/all_to_all | solution.py:96
  35.6 0.8 copy.45
  36.4 5.7 %all-to-all-done.4 = bf16[1,2,4,64,512]{4,3,2,0,1:T(8,128)(2,1)S(1)} async-done(((bf16[1,2,4,64,512]{4,3,2,0,1:T(8,128)(2,1)}), bf16[1,2,4,64,512]{4,3,2,0,1:T(8,128)(2,1)S(1)}, u32[]{:S(2)}, u32[]{:S(2)}) %all-to-all-start.4) | async-done | bytes 524320 | tf_op jit(solution)/shard_map/all_to_all | solution.py:96
  42.1 4.9 %all-to-all-start.1 = ((bf16[1,1,4,128,512]{4,3,1,0,2:T(8,128)(2,1)}), bf16[1,1,4,128,512]{4,3,1,0,2:T(8,128)(2,1)S(1)}, u32[]{:S(2)}, u32[]{:S(2)}) async-start(bf16[1,1,4,128,512]{4,3,1,0,2:T(8,128)(2,1)} %bitcast.5), calls=%async_computation.1 | async-start | bytes 1048576 | tf_op jit(solution)/shard_map/all_to_all | solution.py:102
  47.0 0.0 copy-start.2
  47.0 0.8 copy.49
  47.8 0.0 copy-start.5
  47.8 10.3 %all-to-all-done.1 = bf16[1,1,4,128,512]{4,3,1,0,2:T(8,128)(2,1)S(1)} async-done(((bf16[1,1,4,128,512]{4,3,1,0,2:T(8,128)(2,1)}), bf16[1,1,4,128,512]{4,3,1,0,2:T(8,128)(2,1)S(1)}, u32[]{:S(2)}, u32[]{:S(2)}) %all-to-all-start.1) | async-done | bytes 524320 | tf_op jit(solution)/shard_map/all_to_all | solution.py:102
  58.1 3.5 %all-to-all-start.3 = ((bf16[1,1,4,128,512]{4,3,1,0,2:T(8,128)(2,1)}), bf16[1,1,4,128,512]{4,3,1,0,2:T(8,128)(2,1)S(1)}, u32[]{:S(2)}, u32[]{:S(2)}) async-start(bf16[1,1,4,128,512]{4,3,1,0,2:T(8,128)(2,1)} %bitcast.13), calls=%async_computation.3 | async-start | bytes 1048576 | tf_op jit(solution)/shard_map/all_to_all | solution.py:88
  61.6 0.8 copy.53
  62.5 10.8 %all-to-all-done.3 = bf16[1,1,4,128,512]{4,3,1,0,2:T(8,128)(2,1)S(1)} async-done(((bf16[1,1,4,128,512]{4,3,1,0,2:T(8,128)(2,1)}), bf16[1,1,4,128,512]{4,3,1,0,2:T(8,128)(2,1)S(1)}, u32[]{:S(2)}, u32[]{:S(2)}) %all-to-all-start.3) | async-done | bytes 524320 | tf_op jit(solution)/shard_map/all_to_all | solution.py:88
  73.3 3.5 %all-to-all-start.5 = ((bf16[1,1,4,128,512]{4,3,1,0,2:T(8,128)(2,1)}), bf16[1,1,4,128,512]{4,3,1,0,2:T(8,128)(2,1)S(1)}, u32[]{:S(2)}, u32[]{:S(2)}) async-start(bf16[1,1,4,128,512]{4,3,1,0,2:T(8,128)(2,1)} %bitcast.21), calls=%async_computation.5 | async-start | bytes 1048576 | tf_op jit(solution)/shard_map/all_to_all | solution.py:95
  76.8 0.0 copy-done.2
  76.8 0.1 collective-permute-start
  76.9 2.4 %collective-permute-start.1 = (bf16[64,512]{1,0:T(8,128)(2,1)S(1)}, bf16[64,512]{1,0:T(8,128)(2,1)S(1)}, u32[]{:S(2)}, u32[]{:S(2)}) collective-permute-start(bf16[64,512]{1,0:T(8,128)(2,1)S(1)} %get-tuple-element.34), channel_id=1, source_target_pairs={{0,8},{4,12},{8,0},{12,4},{1,9},{5,13},{9,1},{13,5},{2,10},{6,14},... | collective-permute-start | bytes 196616 | tf_op jit(solution)/shard_map/ppermute | solution.py:25
  79.3 0.1 collective-permute-start.2
  79.4 0.1 copy.63
  80.2 0.0 copy-done.5
  80.2 0.8 sort.17
  81.1 0.5 dynamic_update_slice.15
  81.6 0.0 collective-permute-done
  81.6 0.1 copy.64
  81.8 0.9 dynamic_update_slice.16
  82.7 0.0 collective-permute-done.1
  82.7 0.1 copy.65
  82.8 0.4 dynamic_update_slice.17
  83.2 0.2 collective-permute-done.2
  83.4 0.1 copy.66
  83.5 0.8 dynamic_update_slice.18
  84.4 0.0 copy-start.3
  84.4 0.1 reshape.74
  84.4 0.6 copy-done.3
  85.1 0.6 gather_fusion
  85.6 0.6 gather_fusion.1
  86.2 2.8 %all-to-all-done.5 = bf16[1,1,4,128,512]{4,3,1,0,2:T(8,128)(2,1)S(1)} async-done(((bf16[1,1,4,128,512]{4,3,1,0,2:T(8,128)(2,1)}), bf16[1,1,4,128,512]{4,3,1,0,2:T(8,128)(2,1)S(1)}, u32[]{:S(2)}, u32[]{:S(2)}) %all-to-all-start.5) | async-done | bytes 524320 | tf_op jit(solution)/shard_map/all_to_all | solution.py:95
  89.0 0.6 gather_fusion.2
  89.6 0.2 select_bitcast_fusion.2
  89.9 0.1 squeeze.10
  90.1 0.1 reshape_reshape.8
  90.2 0.7 multiply_reduce_fusion
  90.9 0.0 copy-start
  90.9 0.5 fusion.6
  91.4 0.7 fusion
  92.1 0.7 copy-done
  92.9 0.5 fusion.7
  93.4 0.1 reshape_reshape.7
  93.5 0.0 copy-start.4
  93.5 3.1 %fusion.2 = f32[4,128,512]{2,1,0:T(8,128)S(1)} fusion(f32[4,512,512]{1,2,0:T(8,128)} %copy-done, f32[4,512]{1,0:T(4,128)S(1)} %max.8, bf16[512,4,128]{2,1,0:T(4,128)(2,1)S(1)} %reshape_reshape.7), kind=kOutput, calls=%fused_computation.7 | convolution fusion | flops 271581184 | bytes 5775360 | tf_op jit(solution)/shard_map/while/body/eval_jaxpr/hqk,khd->qhd/dot_general | solution.py:59
  96.7 0.0 copy-done.4
  96.7 0.7 fusion.11
  97.4 0.1 all_to_all.102
  97.5 0.1 copy.68
  97.6 12.3 %all_to_all.116 = bf16[4,128,512]{1,2,0:T(8,128)(2,1)S(1)} all-to-all(bf16[4,128,512]{1,2,0:T(8,128)(2,1)S(1)} %copy.68), channel_id=1, replica_groups=mesh['sect'=2,'seq'=4,'dp'=4] {'seq'}, dimensions={0} | all-to-all | bytes 1048576 | tf_op jit(solution)/shard_map/all_to_all | solution.py:130
  109.9 1.0 copy.69
  (13 shorter events, 0.3 us)
Async XLA Ops:
  0.0 22.7 %copy-start.1 = (bf16[1,8,64,512]{3,2,1,0:T(8,128)(2,1)S(1)}, bf16[1,8,64,512]{3,2,1,0:T(8,128)(2,1)}, u32[]{:S(2)}) copy-start(bf16[1,8,64,512]{3,2,1,0:T(8,128)(2,1)} %param.9) | copy-start | bytes 1572868
  32.1 10.1 %all-to-all-start.4 = ((bf16[1,2,4,64,512]{4,3,2,0,1:T(8,128)(2,1)}), bf16[1,2,4,64,512]{4,3,2,0,1:T(8,128)(2,1)S(1)}, u32[]{:S(2)}, u32[]{:S(2)}) async-start(bf16[1,2,4,64,512]{4,3,2,0,1:T(8,128)(2,1)} %bitcast.17), calls=%async_computation.4 | async-start | bytes 1048576 | tf_op jit(solution)/shard_map/all_to_all | solution.py:96
  42.1 16.0 %all-to-all-start.1 = ((bf16[1,1,4,128,512]{4,3,1,0,2:T(8,128)(2,1)}), bf16[1,1,4,128,512]{4,3,1,0,2:T(8,128)(2,1)S(1)}, u32[]{:S(2)}, u32[]{:S(2)}) async-start(bf16[1,1,4,128,512]{4,3,1,0,2:T(8,128)(2,1)} %bitcast.5), calls=%async_computation.1 | async-start | bytes 1048576 | tf_op jit(solution)/shard_map/all_to_all | solution.py:102
  47.0 29.8 %copy-start.2 = (bf16[1,64,2048]{2,1,0:T(8,128)(2,1)S(1)}, bf16[1,64,2048]{2,1,0:T(8,128)(2,1)}, u32[]{:S(2)}) copy-start(bf16[1,64,2048]{2,1,0:T(8,128)(2,1)} %param.13) | copy-start | bytes 786436
  47.8 32.4 %copy-start.5 = (s32[4]{0:T(128)S(1)}, s32[4]{0:T(128)}, u32[]{:S(2)}) copy-start(s32[4]{0:T(128)} %param.15) | copy-start | bytes 52
  58.1 15.2 %all-to-all-start.3 = ((bf16[1,1,4,128,512]{4,3,1,0,2:T(8,128)(2,1)}), bf16[1,1,4,128,512]{4,3,1,0,2:T(8,128)(2,1)S(1)}, u32[]{:S(2)}, u32[]{:S(2)}) async-start(bf16[1,1,4,128,512]{4,3,1,0,2:T(8,128)(2,1)} %bitcast.13), calls=%async_computation.3 | async-start | bytes 1048576 | tf_op jit(solution)/shard_map/all_to_all | solution.py:88
  73.3 15.7 %all-to-all-start.5 = ((bf16[1,1,4,128,512]{4,3,1,0,2:T(8,128)(2,1)}), bf16[1,1,4,128,512]{4,3,1,0,2:T(8,128)(2,1)S(1)}, u32[]{:S(2)}, u32[]{:S(2)}) async-start(bf16[1,1,4,128,512]{4,3,1,0,2:T(8,128)(2,1)} %bitcast.21), calls=%async_computation.5 | async-start | bytes 1048576 | tf_op jit(solution)/shard_map/all_to_all | solution.py:95
  76.8 4.8 %collective-permute-start = (bf16[64,512]{1,0:T(8,128)(2,1)S(1)}, bf16[64,512]{1,0:T(8,128)(2,1)S(1)}, u32[]{:S(2)}, u32[]{:S(2)}) collective-permute-start(bf16[64,512]{1,0:T(8,128)(2,1)S(1)} %get-tuple-element.23), channel_id=1, source_target_pairs={{0,4},{4,0},{8,12},{12,8},{1,5},{5,1},{9,13},{13,9},{2,6},{6,2},{1... | collective-permute-start | bytes 196616 | tf_op jit(solution)/shard_map/ppermute | solution.py:25
  76.9 5.8 %collective-permute-start.1 = (bf16[64,512]{1,0:T(8,128)(2,1)S(1)}, bf16[64,512]{1,0:T(8,128)(2,1)S(1)}, u32[]{:S(2)}, u32[]{:S(2)}) collective-permute-start(bf16[64,512]{1,0:T(8,128)(2,1)S(1)} %get-tuple-element.34), channel_id=1, source_target_pairs={{0,8},{4,12},{8,0},{12,4},{1,9},{5,13},{9,1},{13,5},{2,10},{6,14},... | collective-permute-start | bytes 196616 | tf_op jit(solution)/shard_map/ppermute | solution.py:25
  79.3 4.0 %collective-permute-start.2 = (bf16[64,512]{1,0:T(8,128)(2,1)S(1)}, bf16[64,512]{1,0:T(8,128)(2,1)S(1)}, u32[]{:S(2)}, u32[]{:S(2)}) collective-permute-start(bf16[64,512]{1,0:T(8,128)(2,1)S(1)} %get-tuple-element.22), channel_id=1, source_target_pairs={{0,12},{4,8},{8,4},{12,0},{1,13},{5,9},{9,5},{13,1},{2,14},{6,10},... | collective-permute-start | bytes 196616 | tf_op jit(solution)/shard_map/ppermute | solution.py:25
  84.4 0.7 copy-start.3
  90.9 1.9 %copy-start = (f32[4,512,512]{1,2,0:T(8,128)}, f32[4,512,512]{1,2,0:T(8,128)S(1)}, u32[]{:S(2)}) copy-start(f32[4,512,512]{1,2,0:T(8,128)S(1)} %get-tuple-element.40) | copy-start | bytes 12582916
  93.5 3.1 %copy-start.4 = (bf16[256,512]{0,1:T(8,128)(2,1)S(1)}, bf16[256,512]{0,1:T(8,128)(2,1)}, u32[]{:S(2)}) copy-start(bf16[256,512]{0,1:T(8,128)(2,1)} %copy-done.3) | copy-start | bytes 786436
